TPU v7x, 32 devices: a whole 2x2x4 slice. The times are simulated.
32 devices in a mesh: groups: 2 (over x), pool: 8 (over z, y), shard: 2 (over core).
Axes of the slice: x: 2, y: 2, z: 4, core: 2. Of those that a mesh axis runs over, the one named last changes fastest.
Arguments:
- tokens: bfloat16 [2, 64, 8192], P(None, ('groups', 'pool'), 'shard'), parts along dimension 1, may hold values from -6 to 6
- counts: int32 [2, 16], P(None, ('groups', 'pool')), parts along dimension 1, may hold values from 0 to 4, as said below
- gate_up: bfloat16 [8192, 2, 28672], P('shard', None, 'pool'), may hold values from -0.0625 to 0.0625
- down: bfloat16 [28672, 8192], P('pool', 'shard'), may hold values from -0.03125 to 0.03125
Outputs:
- mixed: bfloat16 [2, 64, 8192], P(None, ('groups', 'pool'), 'shard'), parts along dimension 1
There are 2 independent parts, one for each index of `groups`. A program takes and returns all parts, laid end to end along the dimension named above; an argument that names none is the same for every part. Nothing has to cross between parts.
Inputs may be any that keep to these rules, and one draw needn't show every extreme that they name: `counts`: in each micro-batch some device has 4 live rows and some has none.
All inputs are finite; a program needn't handle non-finite values.
Results may differ from a plain program's by a relative error of at most 0.005.
Values may be sent and summed in bfloat16 or wider, within the bound.
A program may use at most 256 MiB of HBM per device.

v0:
```python
import jax
import jax.numpy as jnp
from jax import lax
from jax.sharding import PartitionSpec as P


def feed_forward(own_rows, gate_up, down):
    flat_weights = gate_up.reshape(gate_up.shape[0], -1)
    local_units = gate_up.shape[2]
    partial_sums = jnp.dot(
        lax.all_gather(own_rows, "pool", axis=0, tiled=True),
        flat_weights,
        preferred_element_type=jnp.float32,
    )
    row_total = partial_sums.shape[0]
    partial_sums = partial_sums.reshape(row_total, 2, local_units)
    summed = lax.psum(partial_sums, "shard")
    hidden = (jax.nn.silu(summed[:, 0]) * summed[:, 1]).astype(jnp.bfloat16)
    returned = lax.psum_scatter(
        jnp.dot(hidden, down, preferred_element_type=jnp.float32),
        "pool",
        scatter_dimension=0,
        tiled=True,
    )
    return returned.astype(jnp.bfloat16)


def shards(tokens, counts, gate_up, down):
    capacity = tokens.shape[1]
    position = lax.broadcasted_iota(jnp.int32, (capacity, 1), 0)
    nothing = jnp.zeros((), tokens.dtype)
    live_sets = [
        jnp.where(position < counts[micro_batch, 0], tokens[micro_batch], nothing)
        for micro_batch in range(tokens.shape[0])
    ]
    combined = jnp.concatenate(live_sets, axis=0)
    result = feed_forward(combined, gate_up, down)
    stacked = result.reshape(tokens.shape[0], capacity, result.shape[1])
    return stacked


def solution(mesh):
    placed = (
        P(None, ("groups", "pool"), "shard"),
        P(None, ("groups", "pool")),
        P("shard", None, "pool"),
        P("pool", "shard"),
    )
    return jax.shard_map(
        shards,
        mesh=mesh,
        in_specs=placed,
        out_specs=P(None, ("groups", "pool"), "shard"),
        check_vma=False,
    )
```

profile of v0, /device:TPU:0, one launch (start us, length us, event | category | flops | bytes accessed | tf_op | source)
XLA Modules:
  0.0 288.1 jit_solution(295380920429154931)
XLA Ops:
  6.5 0.0 all-reduce.2.cloned.1.call-start
  6.5 39.3 %copy.6 = bf16[512,8,2,3584]{3,1,2,0:T(8,128)(2,1)} copy(bf16[512,8,2,3584]{3,2,1,0:T(2,128)(2,1)} %bitcast.30) | data formatting | bytes 117440512
  45.8 0.0 copy-start.1
  45.8 0.0 copy-start
  45.8 69.5 %copy.5 = bf16[7168,4096]{1,0:T(8,128)(2,1)} copy(bf16[7168,4096]{0,1:T(8,128)(2,1)} %bitcast.29) | data formatting | bytes 117440512 | tf_op jit(solution)/shard_map/dot_general | solution.py:10
  115.3 0.0 copy-done.1
  115.3 0.6 fusion.8
  115.9 1.3 iota_compare_fusion
  117.3 0.0 copy-done
  117.3 0.1 bitcast_select_fusion.1
  117.4 33.0 %all_gather.3 = bf16[64,4096]{1,0:T(8,128)(2,1)S(1)} all-gather(bf16[8,4096]{1,0:T(8,128)(2,1)S(1)} %pad_maximum_fusion), channel_id=1, replica_groups=mesh['groups'=2,'pool'=8,'shard'=2] {'pool'}, dimensions={0}, use_global_device_ids=true | all-gather | bytes 589824 | tf_op jit(solution)/shard_map/all_gather | solution.py:11
  150.5 25.4 %fusion.2 = f32[64,2,3584]{2,0,1:T(8,128)} fusion(bf16[2,3584,4096]{2,1,0:T(8,128)(2,1)} %bitcast.28, bf16[64,4096]{1,0:T(8,128)(2,1)S(1)} %all_gather.3), kind=kOutput, calls=%fused_computation.4 | convolution fusion | flops 3758096384 | bytes 61079552 | tf_op jit(solution)/shard_map/dot_general | solution.py:10
  175.9 0.0 all-reduce.2.cloned.1.call-update
  175.9 0.0 reduce-scatter.2.cloned.1.call-start
  176.0 22.0 %all-reduce.2.cloned.1.call-done = f32[64,2,3584]{2,0,1:T(8,128)} async-done(((f32[64,2,3584]{2,0,1:T(8,128)}), f32[64,2,3584]{2,0,1:T(8,128)}) %all-reduce.2.cloned.1.call-update) | async-done | bytes 1835024 | tf_op jit(solution)/shard_map/psum | solution.py:17
  198.0 16.1 %fusion.4 = f32[64,4096]{1,0:T(8,128)} fusion(bf16[3584,4096]{1,0:T(8,128)(2,1)} %param.7, f32[64,2,3584]{2,0,1:T(8,128)} %all-reduce.2.cloned.1.call-done), kind=kOutput, calls=%fused_computation.6 | convolution fusion | flops 1880424448 | bytes 32243712 | tf_op jit(solution)/shard_map/dot_general | solution.py:20
  214.1 0.0 reduce-scatter.2.cloned.1.call-update
  214.1 65.6 %reduce-scatter.2.cloned.1.call-done = f32[8,4096]{1,0:T(8,128)} async-done(((f32[64,4096]{1,0:T(8,128)}), f32[8,4096]{1,0:T(8,128)}) %reduce-scatter.2.cloned.1.call-update) | async-done | bytes 131088 | tf_op jit(solution)/shard_map/reduce_scatter | solution.py:19
  279.7 0.9 convert_element_type.7
  280.6 0.7 reshape.19
  (1 shorter events, 0.0 us)
Async XLA Ops:
  6.5 191.5 %all-reduce.2.cloned.1.call-start = ((), (), s32[]{:S(2)}) async-start(), calls=%async_computation.1 | async-start | bytes 3670016 | tf_op jit(solution)/shard_map/psum | solution.py:17
  45.8 69.5 %copy-start.1 = (s32[2,1]{0,1:T(1,128)S(1)}, s32[2,1]{0,1:T(1,128)}, u32[]{:S(2)}) copy-start(s32[2,1]{0,1:T(1,128)} %param.5) | copy-start | bytes 28
  45.8 71.5 %copy-start = (bf16[2,4,4096]{2,1,0:T(4,128)(2,1)S(1)}, bf16[2,4,4096]{2,1,0:T(4,128)(2,1)}, u32[]{:S(2)}) copy-start(bf16[2,4,4096]{2,1,0:T(4,128)(2,1)} %param.4) | copy-start | bytes 196612
  175.9 103.8 %reduce-scatter.2.cloned.1.call-start = ((), (), s32[]{:S(2)}) async-start(), calls=%async_computation.2 | async-start | bytes 1179648 | tf_op jit(solution)/shard_map/reduce_scatter | solution.py:19
Sparse Core Ops, SparseCore 0:
  176.0 21.9 all-reduce.1
  214.3 65.3 reduce-scatter.1
where the time goes:
time: 290 us; the launch traced here: 288 us
  local copies, waits for them, and re-layouts  110 us (38%)
  waiting for transfers between devices  87.6 us (30%)
  matrix products  41.5 us (14%)
  blocking collectives  33 us (11%)
  between operations  13.4 us (5%)
    dot_general x1, local copies, waits for them, and re-layouts, feed_forward(): jnp.dot(lax.all_gather(own_rows, 'pool', axis=0, tiled=True), flat_weight...  69.5 us
    reduce_scatter x1, waiting for transfers between devices, feed_forward(): lax.psum_scatter(jnp.dot(hidden, down, preferred_element_type=jnp.float32...  65.6 us
    unnamed x5, local copies, waits for them, and re-layouts  39.3 us
    all_gather x1, blocking collectives, feed_forward(): lax.all_gather(own_rows, 'pool', axis=0, tiled=True)  33 us
    dot_general x1, matrix products, feed_forward(): jnp.dot(lax.all_gather(own_rows, 'pool', axis=0, tiled=True), flat_weight...  25.4 us
    psum x1, waiting for transfers between devices, feed_forward(): summed = lax.psum(partial_sums, 'shard')  22 us
    dot_general x1, matrix products, feed_forward(): jnp.dot(hidden, down, preferred_element_type=jnp.float32)  16.1 us
  transfers between devices with their start and end apart: 2, of which 2 were waited for; matrix products, arithmetic and copies ran while one was open for 0% of the time, Pallas kernels for 0%

commit v1 on v0

v1 whole, which is shorter than its diff:
```python
import functools

import jax
import jax.numpy as jnp
from jax import lax
from jax.experimental import pallas as pl
from jax.experimental.pallas import tpu as pltpu
from jax.sharding import PartitionSpec as P

MESH = pl.DeviceIdType.MESH
F32 = jnp.float32
BF16 = jnp.bfloat16


def layer(
    pool, slow, fast, depth, width, ring, pieces,
    counts_ref, tokens_ref, gate_up_ref, down_ref, out_ref,
    rows_in, rows_wide, sums, sent, got, hidden, gate_buf, down_buf,
    mixed, pair_out, pair_in, slow_out, slow_in,
    own_sem, gate_sem, down_sem,
    rows_send, rows_recv, side_send, side_recv,
    half_send, half_recv, pair_send, pair_recv, slow_send, slow_recv,
):
    micro, capacity, features = tokens_ref.shape
    units = gate_up_ref.shape[2]
    columns = down_ref.shape[1]
    block = micro * capacity
    total = pool * block
    gate_steps = features // depth
    down_steps = columns // width
    me = lax.axis_index("pool")
    core = lax.axis_index("shard")
    at_slow = me // fast
    at_fast = lax.rem(me, fast)
    beside = at_slow * fast + (1 - at_fast)

    def slow_peer(step):
        return lax.rem(at_slow + step, slow)

    def slow_source(step):
        return lax.rem(at_slow + slow - step, slow)

    def gate_copy(step):
        slot = lax.rem(step, ring)
        start = pl.multiple_of(step * depth, depth)
        return pltpu.make_async_copy(
            gate_up_ref.at[pl.ds(start, depth)], gate_buf.at[slot], gate_sem.at[slot]
        )

    def down_copy(step):
        start = pl.multiple_of(step * width, width)
        return pltpu.make_async_copy(
            down_ref.at[:, pl.ds(start, width)], down_buf.at[step], down_sem.at[step]
        )

    own = pltpu.make_async_copy(tokens_ref, rows_in.at[me], own_sem)
    own.start()
    for step in range(ring):
        gate_copy(step).start()

    barrier = pltpu.get_barrier_semaphore()
    for step in range(1, slow):
        pl.semaphore_signal(
            barrier, inc=1, device_id={"pool": slow_peer(step) * fast + at_fast}, device_id_type=MESH
        )
    pl.semaphore_signal(barrier, inc=1, device_id={"pool": beside}, device_id_type=MESH)
    pl.semaphore_signal(barrier, inc=1, device_id={"shard": 1 - core}, device_id_type=MESH)
    pl.semaphore_wait(barrier, slow + 1)

    row_copies = []
    for step in range(1, slow):
        copy = pltpu.make_async_remote_copy(
            src_ref=tokens_ref,
            dst_ref=rows_in.at[me],
            send_sem=rows_send.at[step - 1],
            recv_sem=rows_recv.at[step - 1],
            device_id={"pool": slow_peer(step) * fast + at_fast},
            device_id_type=MESH,
        )
        copy.start()
        row_copies.append(copy)
    first = pltpu.make_async_remote_copy(
        src_ref=tokens_ref,
        dst_ref=rows_in.at[me],
        send_sem=side_send.at[0],
        recv_sem=side_recv.at[0],
        device_id={"pool": beside},
        device_id_type=MESH,
    )
    first.start()
    side_copies = [first]
    sums[...] = jnp.zeros_like(sums)
    for step in range(1, slow):
        row_copies[step - 1].wait_recv()
        source = slow_source(step) * fast + at_fast
        copy = pltpu.make_async_remote_copy(
            src_ref=rows_in.at[source],
            dst_ref=rows_in.at[source],
            send_sem=side_send.at[step],
            recv_sem=side_recv.at[step],
            device_id={"pool": beside},
            device_id_type=MESH,
        )
        copy.start()
        side_copies.append(copy)
    own.wait()
    for copy in side_copies:
        copy.wait()
    for copy in row_copies:
        copy.wait_send()

    lane = lax.broadcasted_iota(jnp.int32, (128, 256), 1)
    place = lax.broadcasted_iota(jnp.int32, (128, 256), 0)
    even = jnp.where(lane == 2 * place, 1.0, 0.0).astype(BF16)
    odd = jnp.where(lane == 2 * place + 1, 1.0, 0.0).astype(BF16)

    def widen(index, carry):
        start = pl.multiple_of(index * 128, 128)
        to = pl.multiple_of(index * 256, 256)
        part = rows_in[:, :, :, pl.ds(start, 128)].reshape(total, 128)
        rows_wide[:total, pl.ds(to, 256)] = jnp.dot(
            part, even, preferred_element_type=F32
        ).astype(BF16)
        rows_wide[total:, pl.ds(to, 256)] = jnp.dot(
            part, odd, preferred_element_type=F32
        ).astype(BF16)
        return carry

    lax.fori_loop(0, features // 128, widen, 0)

    tile = 512

    def project(step, carry):
        gate_copy(step).wait()
        slot = lax.rem(step, ring)
        start = pl.multiple_of(step * 2 * depth, 2 * depth)
        left = rows_wide[:, pl.ds(start, 2 * depth)]
        for at in range(0, units, tile):
            upto = min(at + tile, units)
            weights = gate_buf[slot, :, :, at:upto].reshape(2 * depth, upto - at)
            sums[:, at:upto] += jnp.dot(left, weights, preferred_element_type=F32)

        @pl.when(step + ring < gate_steps)
        def _():
            gate_copy(step + ring).start()

        @pl.when((step + ring >= gate_steps) & (step + ring < gate_steps + down_steps))
        def _():
            down_copy(step + ring - gate_steps).start()

        return carry

    lax.fori_loop(0, gate_steps, project, 0)
    for step in range(ring, down_steps):
        down_copy(step).start()

    span = units // pieces
    halves = []
    for piece in range(pieces):
        at = slice(piece * span, (piece + 1) * span)
        sent[piece] = sums[:, at].astype(BF16)
        copy = pltpu.make_async_remote_copy(
            src_ref=sent.at[piece],
            dst_ref=got.at[piece],
            send_sem=half_send.at[piece],
            recv_sem=half_recv.at[piece],
            device_id={"shard": 1 - core},
            device_id_type=MESH,
        )
        copy.start()
        halves.append(copy)
    for piece in range(pieces):
        at = slice(piece * span, (piece + 1) * span)
        halves[piece].wait()
        gate = sums[:total, at] + got[piece, :total].astype(F32)
        up = sums[total:, at] + got[piece, total:].astype(F32)
        hidden[:, at] = (gate / (1.0 + jnp.exp(-gate)) * up).astype(BF16)

    def pair_copy(step):
        return pltpu.make_async_remote_copy(
            src_ref=pair_out.at[step],
            dst_ref=pair_in.at[step],
            send_sem=pair_send.at[step],
            recv_sem=pair_recv.at[step],
            device_id={"pool": beside},
            device_id_type=MESH,
        )

    def slow_copy(step, ahead):
        return pltpu.make_async_remote_copy(
            src_ref=slow_out.at[step, slow_peer(ahead)],
            dst_ref=slow_in.at[step, ahead - 1],
            send_sem=slow_send.at[step, ahead - 1],
            recv_sem=slow_recv.at[step, ahead - 1],
            device_id={"pool": slow_peer(ahead) * fast + at_fast},
            device_id_type=MESH,
        )

    def spread(step):
        pair_copy(step).wait()
        joined = mixed[step, :, at_fast] + pair_in[step].astype(F32)
        slow_out[step] = joined.astype(BF16)
        for ahead in range(1, slow):
            slow_copy(step, ahead).start()

    def combine(step, carry):
        down_copy(step).wait()
        product = jnp.dot(hidden[...], down_buf[step], preferred_element_type=F32)
        mixed[step] = product.reshape(slow, fast, block, width)
        pair_out[step] = mixed[step, :, 1 - at_fast].astype(BF16)
        pair_copy(step).start()

        @pl.when(step >= 1)
        def _():
            spread(step - 1)

        return carry

    lax.fori_loop(0, down_steps, combine, 0)
    spread(down_steps - 1)

    position = lax.broadcasted_iota(jnp.int32, (capacity, width), 0)

    def finish(step, carry):
        for ahead in range(1, slow):
            slow_copy(step, ahead).wait()
        value = mixed[step, at_slow, at_fast] + pair_in[step, at_slow].astype(F32)
        for ahead in range(1, slow):
            value = value + slow_in[step, ahead - 1].astype(F32)
        start = pl.multiple_of(step * width, width)
        for index in range(micro):
            part = value[index * capacity : (index + 1) * capacity]
            live = position < counts_ref[index, 0]
            out_ref[index, :, pl.ds(start, width)] = jnp.where(live, part, 0.0).astype(BF16)
        return carry

    lax.fori_loop(0, down_steps, finish, 0)


def solution(mesh):
    pool = mesh.shape["pool"]
    fast = 2
    slow = pool // fast
    placed = (
        P(None, ("groups", "pool"), "shard"),
        P(None, ("groups", "pool")),
        P("shard", None, "pool"),
        P("pool", "shard"),
    )

    def shards(tokens, counts, gate_up, down):
        micro, capacity, features = tokens.shape
        units = gate_up.shape[2]
        columns = down.shape[1]
        depth = 256
        width = 512
        ring = 7
        pieces = 4 if units % 512 == 0 else 1
        block = micro * capacity
        total = pool * block
        steps = columns // width
        dma = pltpu.SemaphoreType.DMA
        return pl.pallas_call(
            functools.partial(layer, pool, slow, fast, depth, width, ring, pieces),
            out_shape=jax.ShapeDtypeStruct(tokens.shape, tokens.dtype),
            in_specs=[
                pl.BlockSpec(memory_space=pltpu.SMEM),
                pl.BlockSpec(memory_space=pl.ANY),
                pl.BlockSpec(memory_space=pl.ANY),
                pl.BlockSpec(memory_space=pl.ANY),
            ],
            out_specs=pl.BlockSpec(memory_space=pltpu.VMEM),
            scratch_shapes=[
                pltpu.VMEM((pool, micro, capacity, features), BF16),
                pltpu.VMEM((2 * total, 2 * features), BF16),
                pltpu.VMEM((2 * total, units), F32),
                pltpu.VMEM((pieces, 2 * total, units // pieces), BF16),
                pltpu.VMEM((pieces, 2 * total, units // pieces), BF16),
                pltpu.VMEM((total, units), BF16),
                pltpu.VMEM((ring, depth, 2, units), BF16),
                pltpu.VMEM((steps, units, width), BF16),
                pltpu.VMEM((steps, slow, fast, block, width), F32),
                pltpu.VMEM((steps, slow, block, width), BF16),
                pltpu.VMEM((steps, slow, block, width), BF16),
                pltpu.VMEM((steps, slow, block, width), BF16),
                pltpu.VMEM((steps, slow - 1, block, width), BF16),
                dma,
                dma((ring,)),
                dma((steps,)),
                dma((slow - 1,)),
                dma((slow - 1,)),
                dma((slow,)),
                dma((slow,)),
                dma((pieces,)),
                dma((pieces,)),
                dma((steps,)),
                dma((steps,)),
                dma((steps, slow - 1)),
                dma((steps, slow - 1)),
            ],
            compiler_params=pltpu.CompilerParams(
                collective_id=0, has_side_effects=True, vmem_limit_bytes=67043328
            ),
        )(counts, tokens, gate_up, down)

    return jax.shard_map(
        shards,
        mesh=mesh,
        in_specs=placed,
        out_specs=P(None, ("groups", "pool"), "shard"),
        check_vma=False,
    )
```

time: 290 us -> 62 us (0.21)
  local copies, waits for them, and re-layouts: 110 us -> 2.79 us
  waiting for transfers between devices: 87.6 us -> 0 us
  Pallas kernels: 0 us -> 59 us
  matrix products: 41.5 us -> 0 us
  blocking collectives: 33 us -> 0 us
  between operations: 13.4 us -> 0.01 us
    dot_general x1 -> x0, local copies, waits for them, and re-layouts: 69.5 us -> none  [feed_forward(): jnp.dot(lax.all_gather(own_rows, 'pool', axis=0, tiled=True), flat_weight...]
    reduce_scatter x1 -> x0, waiting for transfers between devices: 65.6 us -> none  [feed_forward(): lax.psum_scatter(jnp.dot(hidden, down, preferred_element_type=jnp.float32...]
    pallas_call x0 -> x1, Pallas kernels: none -> 59 us  [shards(): pl.pallas_call(functools.partial(layer, pool, slow, fast, depth, width, r...]
    dot_general x2 -> x0, matrix products: 41.5 us -> none  [the longest x1 25.4 us: feed_forward(): jnp.dot(lax.all_gather(own_rows, 'pool', axis=0, tiled=True), flat_weight...]
    unnamed x5 -> x2, local copies, waits for them, and re-layouts: 39.3 us -> 2.79 us
    all_gather x1 -> x0, blocking collectives: 33 us -> none  [feed_forward(): lax.all_gather(own_rows, 'pool', axis=0, tiled=True)]
    psum x1 -> x0, waiting for transfers between devices: 22 us -> none  [feed_forward(): summed = lax.psum(partial_sums, 'shard')]
  transfers between devices with their start and end apart: 2 -> 0, of which waited for: 2 -> 0; matrix products, arithmetic and copies ran while one was open for 0% -> 0% of each run, Pallas kernels for 0% -> 0%
where the time goes in v1:
time: 62 us; the launch traced here: 61.8 us
  Pallas kernels  59 us (95%)
  local copies, waits for them, and re-layouts  2.79 us (4%)
    pallas_call x1, Pallas kernels, shards(): pl.pallas_call(functools.partial(layer, pool, slow, fast, depth, width, r...  59 us
    unnamed x2, local copies, waits for them, and re-layouts  2.79 us

profile of v1, /device:TPU:0, one launch (start us, length us, event | category | flops | bytes accessed | tf_op | source)
XLA Modules:
  0.0 61.8 jit_solution(8833769305978928637)
XLA Ops:
  0.0 1.3 %copy.5.counts_ref = s32[2,1]{1,0:T(2,128)} copy(s32[2,1]{0,1:T(1,128)} %param.5) | data formatting | bytes 16 | tf_op args[1]
  1.3 59.0 %shard_map.46 = bf16[2,4,4096]{2,1,0:T(4,128)(2,1)} custom-call(s32[2,1]{1,0:T(2,128)} %copy.5.counts_ref, bf16[2,4,4096]{2,1,0:T(4,128)(2,1)} %tokens_ref.1, bf16[4096,2,3584]{2,1,0:T(2,128)(2,1)} %gate_up_ref.1, bf16[3584,4096]{1,0:T(8,128)(2,1)} %down_ref.1), custom_call_target="tpu_custom_call" | custom-call | tf_op jit(solution)/shard_map/pallas_call | solution.py:263
  60.3 1.5 %copy.7 = bf16[2,4,4096]{2,1,0:T(4,128)(2,1)} copy(bf16[2,4,4096]{2,1,0:T(4,128)(2,1)} %shard_map.46) | data formatting | bytes 131072

commit v2 on v1

--- a/solution.py
+++ b/solution.py
@@ -13,9 +13,9 @@
 
 
 def layer(
-    pool, slow, fast, depth, width, ring, pieces,
+    pool, slow, fast, depth, width, ring, pieces, parts,
     counts_ref, tokens_ref, gate_up_ref, down_ref, out_ref,
-    rows_in, rows_wide, sums, sent, got, hidden, gate_buf, down_buf,
+    rows_in, rows_wide, sums, got, hidden, gate_buf, down_buf,
     mixed, pair_out, pair_in, slow_out, slow_in,
     own_sem, gate_sem, down_sem,
     rows_send, rows_recv, side_send, side_recv,
@@ -67,47 +67,46 @@
     pl.semaphore_signal(barrier, inc=1, device_id={"shard": 1 - core}, device_id_type=MESH)
     pl.semaphore_wait(barrier, slow + 1)
 
-    row_copies = []
-    for step in range(1, slow):
-        copy = pltpu.make_async_remote_copy(
-            src_ref=tokens_ref,
-            dst_ref=rows_in.at[me],
-            send_sem=rows_send.at[step - 1],
-            recv_sem=rows_recv.at[step - 1],
+    half = features // parts
+
+    def row_copy(part, step):
+        at = pl.ds(part * half, half)
+        return pltpu.make_async_remote_copy(
+            src_ref=tokens_ref.at[:, :, at],
+            dst_ref=rows_in.at[me, :, :, at],
+            send_sem=rows_send.at[part, step - 1],
+            recv_sem=rows_recv.at[part, step - 1],
             device_id={"pool": slow_peer(step) * fast + at_fast},
             device_id_type=MESH,
         )
-        copy.start()
-        row_copies.append(copy)
-    first = pltpu.make_async_remote_copy(
-        src_ref=tokens_ref,
-        dst_ref=rows_in.at[me],
-        send_sem=side_send.at[0],
-        recv_sem=side_recv.at[0],
-        device_id={"pool": beside},
-        device_id_type=MESH,
-    )
-    first.start()
-    side_copies = [first]
+
+    def side_copy(part, step):
+        at = pl.ds(part * half, half)
+        source = slow_source(step) * fast + at_fast
+        place = rows_in.at[source, :, :, at]
+        return pltpu.make_async_remote_copy(
+            src_ref=tokens_ref.at[:, :, at] if step == 0 else place,
+            dst_ref=place,
+            send_sem=side_send.at[part, step],
+            recv_sem=side_recv.at[part, step],
+            device_id={"pool": beside},
+            device_id_type=MESH,
+        )
+
+    for part in range(parts):
+        for step in range(1, slow):
+            row_copy(part, step).start()
+        side_copy(part, 0).start()
     sums[...] = jnp.zeros_like(sums)
-    for step in range(1, slow):
-        row_copies[step - 1].wait_recv()
-        source = slow_source(step) * fast + at_fast
-        copy = pltpu.make_async_remote_copy(
-            src_ref=rows_in.at[source],
-            dst_ref=rows_in.at[source],
-            send_sem=side_send.at[step],
-            recv_sem=side_recv.at[step],
-            device_id={"pool": beside},
-            device_id_type=MESH,
-        )
-        copy.start()
-        side_copies.append(copy)
-    own.wait()
-    for copy in side_copies:
-        copy.wait()
-    for copy in row_copies:
-        copy.wait_send()
+
+    def forward(part):
+        for step in range(1, slow):
+            row_copy(part, step).wait()
+            side_copy(part, step).start()
+
+    def arrive(part):
+        for step in range(slow):
+            side_copy(part, step).wait()
 
     lane = lax.broadcasted_iota(jnp.int32, (128, 256), 1)
     place = lax.broadcasted_iota(jnp.int32, (128, 256), 0)
@@ -126,8 +125,6 @@
         ).astype(BF16)
         return carry
 
-    lax.fori_loop(0, features // 128, widen, 0)
-
     tile = 512
 
     def project(step, carry):
@@ -150,18 +147,26 @@
 
         return carry
 
-    lax.fori_loop(0, gate_steps, project, 0)
+    blocks = half // 128
+    share = gate_steps // parts
+    forward(0)
+    own.wait()
+    for part in range(parts):
+        arrive(part)
+        lax.fori_loop(part * blocks, (part + 1) * blocks, widen, 0, unroll=8)
+        if part + 1 < parts:
+            forward(part + 1)
+        lax.fori_loop(part * share, (part + 1) * share, project, 0)
     for step in range(ring, down_steps):
         down_copy(step).start()
 
     span = units // pieces
     halves = []
     for piece in range(pieces):
-        at = slice(piece * span, (piece + 1) * span)
-        sent[piece] = sums[:, at].astype(BF16)
+        at = pl.ds(piece * span, span)
         copy = pltpu.make_async_remote_copy(
-            src_ref=sent.at[piece],
-            dst_ref=got.at[piece],
+            src_ref=sums.at[:, at],
+            dst_ref=got.at[:, at],
             send_sem=half_send.at[piece],
             recv_sem=half_recv.at[piece],
             device_id={"shard": 1 - core},
@@ -172,8 +177,8 @@
     for piece in range(pieces):
         at = slice(piece * span, (piece + 1) * span)
         halves[piece].wait()
-        gate = sums[:total, at] + got[piece, :total].astype(F32)
-        up = sums[total:, at] + got[piece, total:].astype(F32)
+        gate = sums[:total, at] + got[:total, at]
+        up = sums[total:, at] + got[total:, at]
         hidden[:, at] = (gate / (1.0 + jnp.exp(-gate)) * up).astype(BF16)
 
     def pair_copy(step):
@@ -203,6 +208,8 @@
         for ahead in range(1, slow):
             slow_copy(step, ahead).start()
 
+    lag = min(3, down_steps)
+
     def combine(step, carry):
         down_copy(step).wait()
         product = jnp.dot(hidden[...], down_buf[step], preferred_element_type=F32)
@@ -210,14 +217,15 @@
         pair_out[step] = mixed[step, :, 1 - at_fast].astype(BF16)
         pair_copy(step).start()
 
-        @pl.when(step >= 1)
+        @pl.when(step >= lag)
         def _():
-            spread(step - 1)
+            spread(step - lag)
 
         return carry
 
     lax.fori_loop(0, down_steps, combine, 0)
-    spread(down_steps - 1)
+    for step in range(down_steps - lag, down_steps):
+        spread(step)
 
     position = lax.broadcasted_iota(jnp.int32, (capacity, width), 0)
 
@@ -256,12 +264,13 @@
         width = 512
         ring = 7
         pieces = 4 if units % 512 == 0 else 1
+        parts = 2
         block = micro * capacity
         total = pool * block
         steps = columns // width
         dma = pltpu.SemaphoreType.DMA
         return pl.pallas_call(
-            functools.partial(layer, pool, slow, fast, depth, width, ring, pieces),
+            functools.partial(layer, pool, slow, fast, depth, width, ring, pieces, parts),
             out_shape=jax.ShapeDtypeStruct(tokens.shape, tokens.dtype),
             in_specs=[
                 pl.BlockSpec(memory_space=pltpu.SMEM),
@@ -274,8 +283,7 @@
                 pltpu.VMEM((pool, micro, capacity, features), BF16),
                 pltpu.VMEM((2 * total, 2 * features), BF16),
                 pltpu.VMEM((2 * total, units), F32),
-                pltpu.VMEM((pieces, 2 * total, units // pieces), BF16),
-                pltpu.VMEM((pieces, 2 * total, units // pieces), BF16),
+                pltpu.VMEM((2 * total, units), F32),
                 pltpu.VMEM((total, units), BF16),
                 pltpu.VMEM((ring, depth, 2, units), BF16),
                 pltpu.VMEM((steps, units, width), BF16),
@@ -287,10 +295,10 @@
                 dma,
                 dma((ring,)),
                 dma((steps,)),
-                dma((slow - 1,)),
-                dma((slow - 1,)),
-                dma((slow,)),
-                dma((slow,)),
+                dma((parts, slow - 1)),
+                dma((parts, slow - 1)),
+                dma((parts, slow)),
+                dma((parts, slow)),
                 dma((pieces,)),
                 dma((pieces,)),
                 dma((steps,)),

time: 62 us -> 51.7 us (0.83)
  Pallas kernels: 59 us -> 48.7 us
    pallas_call x1, Pallas kernels: 59 us -> 48.7 us  [shards(): pl.pallas_call(functools.partial(layer, pool, slow, fast, depth, width, r...]
where the time goes in v2:
time: 51.7 us; the launch traced here: 51.5 us
  Pallas kernels  48.7 us (94%)
  local copies, waits for them, and re-layouts  2.79 us (5%)
    pallas_call x1, Pallas kernels, shards(): pl.pallas_call(functools.partial(layer, pool, slow, fast, depth, width, r...  48.7 us
    unnamed x2, local copies, waits for them, and re-layouts  2.79 us

profile of v2, /device:TPU:0, one launch (start us, length us, event | category | flops | bytes accessed | tf_op | source)
XLA Modules:
  0.0 51.5 jit_solution(10000804991056347433)
XLA Ops:
  0.0 1.3 %copy.5.counts_ref = s32[2,1]{1,0:T(2,128)} copy(s32[2,1]{0,1:T(1,128)} %param.5) | data formatting | bytes 16 | tf_op args[1]
  1.3 48.7 %shard_map.46 = bf16[2,4,4096]{2,1,0:T(4,128)(2,1)} custom-call(s32[2,1]{1,0:T(2,128)} %copy.5.counts_ref, bf16[2,4,4096]{2,1,0:T(4,128)(2,1)} %tokens_ref.1, bf16[4096,2,3584]{2,1,0:T(2,128)(2,1)} %gate_up_ref.1, bf16[3584,4096]{1,0:T(8,128)(2,1)} %down_ref.1), custom_call_target="tpu_custom_call" | custom-call | tf_op jit(solution)/shard_map/pallas_call | solution.py:272
  50.0 1.5 %copy.7 = bf16[2,4,4096]{2,1,0:T(4,128)(2,1)} copy(bf16[2,4,4096]{2,1,0:T(4,128)(2,1)} %shard_map.46) | data formatting | bytes 131072
